TPU v7x, 512 devices: a whole 4x8x8 slice. The times are simulated.
512 devices in a mesh: rep: 16 (over x, z_lo, core), dp: 32 (over y, z_hi).
Axes of the slice: x: 4, y: 8, z: 8 (z_hi: 4, z_lo: 2; z = z_hi * 2 + z_lo), core: 2. Of those that a mesh axis runs over, the one named last changes fastest.
Arguments:
- image_features: bfloat16 [65536, 1408], P(('rep', 'dp')), parts along dimension 0, may hold values from -24 to 24
- text_embed: bfloat16 [65536, 512], P(('rep', 'dp')), parts along dimension 0, may hold values from -24 to 24
- image_head: bfloat16 [22528, 512], P(('rep', 'dp')), parts along dimension 0, may hold values from -1 to 3
- logit_scale: float32 [1], replicated, may hold values from 10 to 40
Outputs:
- image_features_grad: bfloat16 [65536, 1408], P(('rep', 'dp')), parts along dimension 0
- text_embed_grad: bfloat16 [65536, 512], P(('rep', 'dp')), parts along dimension 0
- image_head_grad: float32 [22528, 512], P(('rep', 'dp')), parts along dimension 0
There are 16 independent parts, one for each index of `rep`. A program takes and returns all parts, laid end to end along the dimension named above; an argument that names none is the same for every part. Nothing has to cross between parts.
All inputs are finite; a program needn't handle non-finite values.
Results may differ from a plain program's by a relative error of at most 0.02.
Values may be sent and summed in bfloat16 or wider, within the bound.
No kernel may reach another device: no remote copies, remote signals or barrier semaphores. Data moves between devices by JAX's collectives and lax.ppermute only.
A program may use at most 64 MiB of HBM per device.

v0:
```python
import jax
import jax.numpy as jnp
from jax import lax
from jax.sharding import Mesh
from jax.sharding import PartitionSpec as P

DP = ("dp_0", "dp_1")
REP_DP = ("rep", "dp_0", "dp_1")


def from_everyone(array, axis):
    devices = lax.axis_size(axis)
    return lax.all_to_all(
        jnp.broadcast_to(array[None], (devices, *array.shape)), axis, 0, 0, tiled=True
    )


def joined_along(parts, dim):
    shape = list(parts.shape[1:])
    shape[dim] *= parts.shape[0]
    return jnp.moveaxis(parts, 0, dim).reshape(shape)


def collect(array, axis, dim):
    parts = from_everyone(array, axis)
    return joined_along(parts, dim)


def gathered_by_axis(array, axes, dim):
    if not axes:
        return array
    nearer = lax.all_gather(array, axes[-1], axis=dim, tiled=True)
    return gathered_by_axis(nearer, axes[:-1], dim)


def split_up(array, dim, devices):
    before, after = (array.shape[:dim], array.shape[dim + 1 :])
    return jnp.moveaxis(array.reshape(*before, devices, -1, *after), dim, 0)


def sent_and_summed(array, axis, dim):
    devices = lax.axis_size(axis)
    parts = lax.all_to_all(split_up(array, dim, devices), axis, 0, 0, tiled=True)
    return jnp.sum(parts, axis=0)


def rows_first(arrays, axis, dims):
    turned = [jnp.moveaxis(a, dim, 0) for a, dim in zip(arrays, dims)]
    widths = [t[0].size for t in turned]
    both = jnp.concatenate([t.reshape(-1, w) for t, w in zip(turned, widths)], axis=1)
    result = lax.all_gather(both, axis, axis=0, tiled=True)
    parts = jnp.split(result, [sum(widths[:k]) for k in range(1, len(widths))], axis=1)
    return tuple(
        (
            jnp.moveaxis(b.reshape(-1, *t.shape[1:]), 0, dim)
            for b, t, dim in zip(parts, turned, dims)
        )
    )


def summed_on_arrival(array, axis, dim):
    devices = lax.axis_size(axis)
    parts = lax.all_to_all(split_up(array, dim, devices), axis, 0, 0, tiled=True)
    return jnp.sum(parts.astype(jnp.float32), axis=0)


def unit_rows(embedding):
    inv_norm = lax.rsqrt(jnp.sum(embedding * embedding, axis=1, keepdims=True) + 1e-06)
    return (embedding * inv_norm, inv_norm)


def norm_backward(embedding, inv_norm, upstream):
    inner = jnp.sum(embedding * upstream, axis=1, keepdims=True)
    return (inv_norm * upstream - embedding * (inv_norm * inv_norm * inv_norm) * inner).astype(
        jnp.bfloat16
    )


def tile_logits(logit_mult, left_rows, right_rows):
    product = lax.dot_general(
        left_rows, right_rows, (((1,), (1,)), ((), ())), preferred_element_type=jnp.float32
    )
    return logit_mult * product


def pair_coef(logits, left_lse, right_lse, left_ids, right_ids):
    label = (left_ids[:, None] == right_ids[None, :]).astype(jnp.float32)
    values = (
        jnp.exp(logits - left_lse[:, None]) + jnp.exp(logits - right_lse[None, :]) - 2.0 * label
    )
    return values.astype(jnp.bfloat16)


def local(image_features, text_embed, image_head, logit_scale):
    logit_mult = logit_scale[0]
    row_count = image_features.shape[0]
    batch_total = row_count * lax.axis_size(DP)
    own_ids = lax.axis_index(DP) * row_count + jnp.arange(row_count, dtype=jnp.int32)
    head_full = collect(image_head, DP, 0)
    img_emb = jnp.dot(image_features, head_full, preferred_element_type=jnp.float32)
    img_scaled, img_inv = unit_rows(img_emb)
    img_unit = img_scaled.astype(jnp.bfloat16)
    txt_emb = text_embed.astype(jnp.float32)
    txt_scaled, txt_inv = unit_rows(txt_emb)
    txt_unit = txt_scaled.astype(jnp.bfloat16)
    text_all = gathered_by_axis(txt_unit, DP, 0)
    exp_tile = jnp.exp(tile_logits(logit_mult, img_unit, text_all))
    col_part = jnp.sum(exp_tile, axis=0)
    row_sum, col_part = (jnp.sum(exp_tile, axis=1), col_part)
    row_lse = jnp.log(row_sum)
    col_lse = jnp.log(sent_and_summed(col_part, DP, 0))
    row_all, col_all = rows_first((row_lse, col_lse), DP, (0, 0))
    all_ids = jnp.arange(batch_total, dtype=jnp.int32)
    img_coef = pair_coef(
        tile_logits(logit_mult, img_unit, text_all), row_lse, col_all, own_ids, all_ids
    )
    img_sum = jnp.dot(img_coef, text_all, preferred_element_type=jnp.float32)
    units = lax.all_gather(img_unit, DP, axis=0, tiled=True)
    piece_ids = jnp.arange(units.shape[0], dtype=jnp.int32)
    txt_coef = pair_coef(
        tile_logits(logit_mult, txt_unit, units), col_lse, row_all, own_ids, piece_ids
    )
    txt_sum = jnp.dot(txt_coef, units, preferred_element_type=jnp.float32)
    img_unit_grad = logit_mult * img_sum
    txt_unit_grad = logit_mult * txt_sum
    img_emb_grad = norm_backward(img_emb, img_inv, img_unit_grad)
    text_embed_grad = norm_backward(txt_emb, txt_inv, txt_unit_grad)
    image_features_grad = lax.dot_general(
        img_emb_grad, head_full, (((1,), (1,)), ((), ())), preferred_element_type=jnp.float32
    ).astype(jnp.bfloat16)
    head_partial = lax.dot_general(
        image_features, img_emb_grad, (((0,), (0,)), ((), ())), preferred_element_type=jnp.float32
    )
    image_head_grad = summed_on_arrival(head_partial.astype(jnp.bfloat16), DP, 0)
    return (image_features_grad, text_embed_grad, image_head_grad)


def solution(mesh):
    split = Mesh(mesh.devices.reshape(mesh.shape["rep"], 8, 4), ("rep", "dp_0", "dp_1"))
    return jax.shard_map(
        local,
        mesh=split,
        in_specs=(P(REP_DP, None), P(REP_DP, None), P(REP_DP, None), P()),
        out_specs=(P(REP_DP, None), P(REP_DP, None), P(REP_DP, None)),
        check_vma=False,
    )
```

profile of v0, /device:TPU:6, one launch (start us, length us, event | category | flops | bytes accessed | tf_op | source)
XLA Modules:
  0.0 281.0 jit_solution(6966936409692230886)
XLA Ops:
  7.2 0.0 copy-start
  7.2 0.0 all-gather.3.cloned.1.call-start
  7.2 1.1 fusion.9
  8.3 1.0 fusion.10
  9.3 0.0 copy-start.3
  9.3 22.3 %all_gather.12 = bf16[512,512]{1,0:T(8,128)(2,1)} all-gather(bf16[128,512]{1,0:T(8,128)(2,1)S(1)} %fusion.10), channel_id=1, replica_groups=mesh['rep'=16,'dp_0'=8,'dp_1'=4] {'dp_1'}, dimensions={0}, use_global_device_ids=true | all-gather | bytes 655360 | tf_op jit(solution)/shard_map/all_gather | solution.py:32
  31.6 0.0 all-gather.3.cloned.1.call-update
  31.6 0.0 all-gather.5.cloned.1.call-start
  31.7 1.0 broadcast_in_dim.2
  32.6 0.0 copy-done.3
  32.6 64.9 %all_to_all.19 = bf16[32,44,512]{2,1,0:T(8,128)(2,1)S(1)} all-to-all(bf16[32,44,512]{2,1,0:T(8,128)(2,1)S(1)} %broadcast_in_dim.2), channel_id=1, replica_groups=mesh['rep'=16,'dp_0'=8,'dp_1'=4] {'dp_0','dp_1'}, dimensions={0} | all-to-all | bytes 2883584 | tf_op jit(solution)/shard_map/all_to_all | solution.py:13
  97.6 0.3 reshape.67
  97.9 0.0 copy-done
  97.9 0.5 multiply_reduce_fusion.1
  98.4 0.8 multiply_convert_fusion
  99.1 0.0 all-gather.5.cloned.1.call-update
  99.8 17.5 %all-gather.3.cloned.1.call-done = bf16[4096,512]{1,0:T(8,128)(2,1)} async-done(((bf16[512,512]{1,0:T(8,128)(2,1)}), bf16[4096,512]{1,0:T(8,128)(2,1)}) %all-gather.3.cloned.1.call-update) | async-done | bytes 4194320 | tf_op jit(solution)/shard_map/all_gather | solution.py:32
  117.3 5.7 %exponential_reduce_fusion.1 = (f32[128]{0:T(128)S(1)}, f32[4096]{0:T(1024)}, f32[128,4096]{1,0:T(8,128)}) fusion(bf16[128,512]{1,0:T(8,128)(2,1)} %multiply_convert_fusion, bf16[4096,512]{1,0:T(8,128)(2,1)} %all-gather.3.cloned.1.call-done, f32[]{:T(128)} %bitcast.24), kind=kOutput, calls=%fused_computation.12 | convolution fusion | flops 538439552 | bytes 6439428 | tf_op jit(solution)/shard_map/dot_general | solution.py:80
  123.0 9.7 %all-to-all-start.1 = ((f32[32,1,128]{2,1,0:T(1,128)}), f32[32,1,128]{2,1,0:T(1,128)S(1)}, u32[]{:S(2)}, u32[]{:S(2)}) async-start(f32[32,1,128]{2,1,0:T(1,128)} %bitcast.2), calls=%async_computation.1 | async-start | bytes 32768 | tf_op jit(solution)/shard_map/all_to_all | solution.py:43
  132.7 12.1 %all-to-all-done.1 = f32[32,1,128]{2,1,0:T(1,128)S(1)} async-done(((f32[32,1,128]{2,1,0:T(1,128)}), f32[32,1,128]{2,1,0:T(1,128)S(1)}, u32[]{:S(2)}, u32[]{:S(2)}) %all-to-all-start.1) | async-done | bytes 16416 | tf_op jit(solution)/shard_map/all_to_all | solution.py:43
  144.9 76.4 %all_gather.14 = f32[4096,2]{0,1:T(2,128)S(1)} all-gather(f32[128,2]{0,1:T(2,128)S(1)} %pad_maximum_fusion), channel_id=1, replica_groups=mesh['rep'=16,'dp_0'=8,'dp_1'=4] {'dp_0','dp_1'}, dimensions={0}, use_global_device_ids=true | all-gather | bytes 33792 | tf_op jit(solution)/shard_map/all_gather | solution.py:51
  221.3 3.9 %multiply_reduce_fusion = (f32[128]{0:T(128)S(1)}, f32[128,512]{1,0:T(8,128)S(1)}) fusion(f32[128,512]{1,0:T(8,128)S(1)} %get-tuple-element.16, bf16[4096,512]{1,0:T(8,128)(2,1)} %all-gather.3.cloned.1.call-done, f32[128,4096]{1,0:T(8,128)} %get-tuple-element.17, s32[128]{0:T(128)S(1)} %iota_add_fusion, f32[4096]{0:T(1024)S(1)} %bitcast.28, ...), kind=kOutput, calls=%fused_computation.31 | convolution fusion | flops 540737408 | bytes 6833668 | tf_op jit(solution)/shard_map/dot_general | solution.py:117
  225.2 0.1 subtract_convert_fusion
  225.3 0.0 copy-start.2
  225.3 0.6 copy-done.2
  226.0 1.7 fusion
  227.6 1.7 copy.10
  229.3 1.3 reshape.68
  230.6 5.2 %all-to-all-start.2 = ((bf16[32,44,512]{2,1,0:T(8,128)(2,1)}), bf16[32,44,512]{2,1,0:T(8,128)(2,1)S(1)}, u32[]{:S(2)}, u32[]{:S(2)}) async-start(bf16[32,44,512]{2,1,0:T(8,128)(2,1)} %reshape.68), calls=%async_computation.2 | async-start | bytes 3145728 | tf_op jit(solution)/shard_map/all_to_all | solution.py:63
  235.9 0.0 copy-start.1
  235.9 2.3 convolution_convert_fusion.1
  238.2 28.6 %all-to-all-done.2 = bf16[32,44,512]{2,1,0:T(8,128)(2,1)S(1)} async-done(((bf16[32,44,512]{2,1,0:T(8,128)(2,1)}), bf16[32,44,512]{2,1,0:T(8,128)(2,1)S(1)}, u32[]{:S(2)}, u32[]{:S(2)}) %all-to-all-start.2) | async-done | bytes 1441824 | tf_op jit(solution)/shard_map/all_to_all | solution.py:63
  266.8 0.9 convert_reduce_fusion
  267.7 0.0 all-gather.5.cloned.1.call-done
  267.7 0.0 copy-done.1
  267.7 5.7 %fusion.14 = (f32[128]{0:T(128)S(1)}, f32[128,512]{1,0:T(8,128)S(1)}) fusion(bf16[128,512]{1,0:T(8,128)(2,1)S(1)} %copy-done.1, bf16[4096,512]{1,0:T(8,128)(2,1)} %all-gather.5.cloned.1.call-done, bf16[128,512]{1,0:T(8,128)(2,1)} %copy-done.3, f32[4096]{0:T(1024)S(1)} %bitcast.27, f32[128]{0:T(128)S(1)} %get-tuple-element.9, s32[128]{0:T(128)S(1)} %iota_add_fusion, ...), kind=kOutput, calls=%fused_computation.29 | convolution fusion | flops 1078198144 | bytes 4736516 | tf_op jit(solution)/shard_map/dot_general | solution.py:123
  273.3 0.8 fusion.13
  (8 shorter events, 0.1 us)
Async XLA Ops:
  7.2 90.7 %copy-start = (bf16[128,1408]{1,0:T(8,128)(2,1)S(1)}, bf16[128,1408]{1,0:T(8,128)(2,1)}, u32[]{:S(2)}) copy-start(bf16[128,1408]{1,0:T(8,128)(2,1)} %param.4) | copy-start | bytes 1081348
  7.2 110.1 %all-gather.3.cloned.1.call-start = ((), (), s32[]{:S(2)}) async-start(), calls=%async_computation.3 | async-start | bytes 4718592 | tf_op jit(solution)/shard_map/all_gather | solution.py:32
  9.3 23.3 %copy-start.3 = (bf16[128,512]{1,0:T(8,128)(2,1)}, bf16[128,512]{1,0:T(8,128)(2,1)S(1)}, u32[]{:S(2)}) copy-start(bf16[128,512]{1,0:T(8,128)(2,1)S(1)} %fusion.10) | copy-start | bytes 393220
  31.6 236.1 %all-gather.5.cloned.1.call-start = ((), (), s32[]{:S(2)}) async-start(), calls=%async_computation.4 | async-start | bytes 4325376 | tf_op jit(solution)/shard_map/all_gather | solution.py:118
  123.0 21.8 %all-to-all-start.1 = ((f32[32,1,128]{2,1,0:T(1,128)}), f32[32,1,128]{2,1,0:T(1,128)S(1)}, u32[]{:S(2)}, u32[]{:S(2)}) async-start(f32[32,1,128]{2,1,0:T(1,128)} %bitcast.2), calls=%async_computation.1 | async-start | bytes 32768 | tf_op jit(solution)/shard_map/all_to_all | solution.py:43
  225.3 0.7 copy-start.2
  230.6 36.1 %all-to-all-start.2 = ((bf16[32,44,512]{2,1,0:T(8,128)(2,1)}), bf16[32,44,512]{2,1,0:T(8,128)(2,1)S(1)}, u32[]{:S(2)}, u32[]{:S(2)}) async-start(bf16[32,44,512]{2,1,0:T(8,128)(2,1)} %reshape.68), calls=%async_computation.2 | async-start | bytes 3145728 | tf_op jit(solution)/shard_map/all_to_all | solution.py:63
  235.9 31.8 %copy-start.1 = (bf16[128,512]{1,0:T(8,128)(2,1)S(1)}, bf16[128,512]{1,0:T(8,128)(2,1)}, u32[]{:S(2)}) copy-start(bf16[128,512]{1,0:T(8,128)(2,1)} %param.5) | copy-start | bytes 393220
Sparse Core Ops, SparseCore 0:
  31.7 85.5 all-gather.2
  121.0 101.9 all-gather.4
where the time goes:
time: 281 us
  blocking collectives  164 us (58%)
  waiting for transfers between devices  58.2 us (21%)
  matrix products  19.7 us (7%)
  starting transfers between devices  15 us (5%)
  between operations  14.8 us (5%)
  local copies, waits for them, and re-layouts  4.97 us (2%)
  other arithmetic  4.66 us (2%)
    all_gather x1, blocking collectives, rows_first(): result = lax.all_gather(both, axis, axis=0, tiled=True)  76.4 us
    all_to_all x1, blocking collectives, from_everyone(): lax.all_to_all(jnp.broadcast_to(array[None], (devices, *array.shape)), ax...  64.9 us
    all_to_all x1, waiting for transfers between devices, summed_on_arrival(): lax.all_to_all(split_up(array, dim, devices), axis, 0, 0, tiled=True)  28.6 us
    all_gather x1, blocking collectives, gathered_by_axis(): nearer = lax.all_gather(array, axes[-1], axis=dim, tiled=True)  22.3 us
    all_gather x1, waiting for transfers between devices, gathered_by_axis(): nearer = lax.all_gather(array, axes[-1], axis=dim, tiled=True)  17.5 us
    all_to_all x1, waiting for transfers between devices, sent_and_summed(): lax.all_to_all(split_up(array, dim, devices), axis, 0, 0, tiled=True)  12.1 us
    all_to_all x1, starting transfers between devices, sent_and_summed(): lax.all_to_all(split_up(array, dim, devices), axis, 0, 0, tiled=True)  9.68 us
    dot_general x1, matrix products, tile_logits(): lax.dot_general(left_rows, right_rows, (((1,), (1,)), ((), ())), preferre...  5.75 us
  transfers between devices with their start and end apart: 4, of which 3 were waited for; matrix products, arithmetic and copies ran while one was open for 7% of the time, Pallas kernels for 0%

commit v1 on v0

v1 whole, which is shorter than its diff:
```python
import jax
import jax.numpy as jnp
from jax import lax
from jax.sharding import Mesh
from jax.sharding import PartitionSpec as P

NY, NZ = 8, 4
Y, Z = "dp_0", "dp_1"
DP = (Y, Z)


def to_all(array, axis, devices):
    copies = jnp.broadcast_to(array[None], (devices, *array.shape))
    return lax.all_to_all(copies, axis, 0, 0, tiled=True)


def inv_norm(embedding):
    return lax.rsqrt(jnp.sum(embedding * embedding, axis=1, keepdims=True) + 1e-06)


def norm_backward(embedding, inv, upstream):
    inner = jnp.sum(embedding * upstream, axis=1, keepdims=True)
    return (inv * upstream - embedding * (inv * inv * inv) * inner).astype(jnp.bfloat16)


def own_and_sent(partial, received, own, devices):
    rows = partial.shape[0] // devices
    mine = lax.dynamic_slice_in_dim(partial, own * rows, rows, 0)
    ids = jnp.arange(devices, dtype=jnp.int32)[:, None, None]
    others = jnp.where(ids == own, 0.0, received.astype(jnp.float32))
    return jnp.sum(others, axis=0) + mine


def local(image_features, text_embed, image_head, logit_scale):
    scale = logit_scale[0]
    rows = image_features.shape[0]
    a, b = lax.axis_index(Y), lax.axis_index(Z)

    head_parts = to_all(image_head, DP, NY * NZ)
    head = head_parts.reshape(-1, head_parts.shape[-1])

    txt_emb = text_embed.astype(jnp.float32)
    txt_inv = inv_norm(txt_emb)
    txt_unit = (txt_emb * txt_inv).astype(jnp.bfloat16)
    texts = to_all(txt_unit, Y, NY).reshape(NY * rows, -1)

    img_emb = jnp.dot(image_features, head, preferred_element_type=jnp.float32)
    img_inv = inv_norm(img_emb)
    img_unit = (img_emb * img_inv).astype(jnp.bfloat16)
    images = to_all(img_unit, Z, NZ).reshape(NZ * rows, -1)

    logits = scale * lax.dot_general(
        images, texts, (((1,), (1,)), ((), ())), preferred_element_type=jnp.float32
    )
    exps = jnp.exp(logits)
    row_part = jnp.sum(exps, axis=1)
    col_part = jnp.sum(exps, axis=0)

    wide = jnp.pad(row_part, (0, col_part.shape[0] - row_part.shape[0]))
    same_col = (jnp.arange(NZ, dtype=jnp.int32) == b)[None, :, None]
    same_row = (jnp.arange(NY, dtype=jnp.int32) == a)[:, None, None]
    sums = jnp.where(same_col, col_part[None, None, :], jnp.where(same_row, wide[None, None, :], 0.0))
    sums = lax.all_to_all(sums.reshape(NY * NZ, -1), DP, 0, 0, tiled=True).reshape(NY, NZ, -1)
    col_sum = jnp.sum(jnp.where(same_col, sums, 0.0), axis=(0, 1))
    row_sum = jnp.sum(jnp.where(same_row & ~same_col, sums, 0.0), axis=(0, 1))
    row_sum = row_sum[: NZ * rows] + row_part

    i = jnp.arange(NZ * rows, dtype=jnp.int32) - b * rows
    j = jnp.arange(NY * rows, dtype=jnp.int32) - a * rows
    own_i = (i >= 0) & (i < rows)
    label = (i[:, None] == j[None, :]) & own_i[:, None]
    coef = exps * ((1.0 / row_sum)[:, None] + (1.0 / col_sum)[None, :])
    coef = (coef - jnp.where(label, 2.0, 0.0)).astype(jnp.bfloat16)

    img_part = jnp.dot(coef, texts, preferred_element_type=jnp.float32)
    txt_part = lax.dot_general(
        coef, images, (((0,), (0,)), ((), ())), preferred_element_type=jnp.float32
    )
    img_sent = lax.all_to_all(
        img_part.astype(jnp.bfloat16).reshape(NZ, rows, -1), Z, 0, 0, tiled=True
    )
    txt_sent = lax.all_to_all(
        txt_part.astype(jnp.bfloat16).reshape(NY, rows, -1), Y, 0, 0, tiled=True
    )
    img_unit_grad = scale * own_and_sent(img_part, img_sent, b, NZ)
    img_emb_grad = norm_backward(img_emb, img_inv, img_unit_grad)
    head_part = lax.dot_general(
        image_features, img_emb_grad, (((0,), (0,)), ((), ())), preferred_element_type=jnp.float32
    ).astype(jnp.bfloat16)
    head_sent = lax.all_to_all(
        head_part.reshape(NY * NZ, -1, head_part.shape[-1]), DP, 0, 0, tiled=True
    )
    image_features_grad = lax.dot_general(
        img_emb_grad, head, (((1,), (1,)), ((), ())), preferred_element_type=jnp.float32
    ).astype(jnp.bfloat16)
    txt_unit_grad = scale * own_and_sent(txt_part, txt_sent, a, NY)
    text_embed_grad = norm_backward(txt_emb, txt_inv, txt_unit_grad)
    image_head_grad = jnp.sum(head_sent.astype(jnp.float32), axis=0)
    return (image_features_grad, text_embed_grad, image_head_grad)


def solution(mesh):
    split = Mesh(mesh.devices.reshape(mesh.shape["rep"], NY, NZ), ("rep", Y, Z))
    spec = P(("rep", Y, Z), None)
    return jax.shard_map(
        local,
        mesh=split,
        in_specs=(spec, spec, spec, P(None)),
        out_specs=(spec, spec, spec),
        check_vma=False,
    )
```

time: 281 us -> 240 us (0.85)
  blocking collectives: 164 us -> 0 us
  waiting for transfers between devices: 58.2 us -> 157 us
  starting transfers between devices: 15 us -> 46.8 us
  between operations: 14.8 us -> 1.55 us
  other arithmetic: 4.66 us -> 10.4 us
  matrix products: 19.7 us -> 14.5 us
  local copies, waits for them, and re-layouts: 4.97 us -> 8.6 us
    all_to_all x2 -> x7, waiting for transfers between devices: 40.7 us -> 157 us  [the longest x3 82.9 us: to_all(): return lax.all_to_all(copies, axis, 0, 0, tiled=True)]
    all_gather x2 -> x0, blocking collectives: 98.7 us -> none  [the longest x1 76.4 us: rows_first(): result = lax.all_gather(both, axis, axis=0, tiled=True)]
    all_to_all x1 -> x0, blocking collectives: 64.9 us -> none  [from_everyone(): lax.all_to_all(jnp.broadcast_to(array[None], (devices, *array.shape)), ax...]
    all_to_all x2 -> x7, starting transfers between devices: 14.9 us -> 46.8 us  [the longest x3 28.3 us: to_all(): return lax.all_to_all(copies, axis, 0, 0, tiled=True)]
    all_gather x2 -> x0, waiting for transfers between devices: 17.5 us -> none  [the longest x1 17.5 us: gathered_by_axis(): nearer = lax.all_gather(array, axes[-1], axis=dim, tiled=True)]
    dot_general x5, matrix products: 18 us -> 12.9 us  [the longest x1 3.57 us: local(): lax.dot_general(images, texts, (((1,), (1,)), ((), ())), preferred_elemen...]
    broadcast_in_dim x1 -> x7, local copies, waits for them, and re-layouts: 0.97 us -> 4.39 us  [the longest x3 4.1 us: to_all(): copies = jnp.broadcast_to(array[None], (devices, *array.shape))]
    reduce_sum x3 -> x7, other arithmetic: 1.96 us -> 5.1 us  [the longest x2 2.77 us: own_and_sent(): return jnp.sum(others, axis=0) + mine]
  transfers between devices with their start and end apart: 4 -> 7, of which waited for: 3 -> 7; matrix products, arithmetic and copies ran while one was open for 7% -> 7% of each run, Pallas kernels for 0% -> 0%
where the time goes in v1:
time: 240 us; the launch traced here: 239 us
  waiting for transfers between devices  157 us (65%)
  starting transfers between devices  46.8 us (20%)
  matrix products  14.5 us (6%)
  other arithmetic  10.4 us (4%)
  local copies, waits for them, and re-layouts  8.6 us (4%)
    all_to_all x3, waiting for transfers between devices, to_all(): return lax.all_to_all(copies, axis, 0, 0, tiled=True)  82.9 us
    all_to_all x1, waiting for transfers between devices, local(): lax.all_to_all(head_part.reshape(NY * NZ, -1, head_part.shape[-1]), DP, 0...  33.8 us
    all_to_all x3, starting transfers between devices, to_all(): return lax.all_to_all(copies, axis, 0, 0, tiled=True)  28.3 us
    all_to_all x1, waiting for transfers between devices, local(): lax.all_to_all(txt_part.astype(jnp.bfloat16).reshape(NY, rows, -1), Y, 0,...  19 us
    all_to_all x1, waiting for transfers between devices, local(): lax.all_to_all(sums.reshape(NY * NZ, -1), DP, 0, 0, tiled=True)  12.1 us
    all_to_all x1, waiting for transfers between devices, local(): lax.all_to_all(img_part.astype(jnp.bfloat16).reshape(NZ, rows, -1), Z, 0,...  9.61 us
    all_to_all x1, starting transfers between devices, local(): lax.all_to_all(head_part.reshape(NY * NZ, -1, head_part.shape[-1]), DP, 0...  5.32 us
    all_to_all x1, starting transfers between devices, local(): lax.all_to_all(sums.reshape(NY * NZ, -1), DP, 0, 0, tiled=True)  4.81 us
  transfers between devices with their start and end apart: 7, of which 7 were waited for; matrix products, arithmetic and copies ran while one was open for 7% of the time, Pallas kernels for 0%

profile of v1, /device:TPU:6, one launch (start us, length us, event | category | flops | bytes accessed | tf_op | source)
XLA Modules:
  0.0 239.2 jit_solution(6737936411353474302)
XLA Ops:
  0.6 0.0 copy-start
  0.6 0.0 copy-start.3
  0.7 2.2 broadcast_in_dim.137
  2.8 16.0 %all-to-all-start = ((bf16[32,44,512]{2,1,0:T(8,128)(2,1)}), bf16[32,44,512]{2,1,0:T(8,128)(2,1)S(1)}, u32[]{:S(2)}, u32[]{:S(2)}) async-start(bf16[32,44,512]{2,1,0:T(8,128)(2,1)} %broadcast_in_dim.137), calls=%async_computation | async-start | bytes 3145728 | tf_op jit(solution)/shard_map/all_to_all | solution.py:14
  18.8 0.0 copy-done.3
  18.8 0.1 fusion.1
  18.9 0.1 fusion.2
  19.1 40.4 %all-to-all-done = bf16[32,44,512]{2,1,0:T(8,128)(2,1)S(1)} async-done(((bf16[32,44,512]{2,1,0:T(8,128)(2,1)}), bf16[32,44,512]{2,1,0:T(8,128)(2,1)S(1)}, u32[]{:S(2)}, u32[]{:S(2)}) %all-to-all-start) | async-done | bytes 1441824 | tf_op jit(solution)/shard_map/all_to_all | solution.py:14
  59.5 1.1 broadcast_in_dim.141
  60.6 8.8 %all-to-all-start.2 = ((bf16[8,128,512]{2,1,0:T(8,128)(2,1)}), bf16[8,128,512]{2,1,0:T(8,128)(2,1)}, u32[]{:S(2)}, u32[]{:S(2)}) async-start(bf16[8,128,512]{2,1,0:T(8,128)(2,1)} %broadcast_in_dim.141), calls=%async_computation.2 | async-start | bytes 2097152 | tf_op jit(solution)/shard_map/all_to_all | solution.py:14
  69.4 0.3 reshape.211
  69.7 0.0 copy-done
  69.7 0.5 multiply_reduce_fusion.1
  70.2 0.1 multiply_convert_fusion
  70.3 28.1 %all-to-all-done.2 = bf16[8,128,512]{2,1,0:T(8,128)(2,1)} async-done(((bf16[8,128,512]{2,1,0:T(8,128)(2,1)}), bf16[8,128,512]{2,1,0:T(8,128)(2,1)}, u32[]{:S(2)}, u32[]{:S(2)}) %all-to-all-start.2) | async-done | bytes 1048608 | tf_op jit(solution)/shard_map/all_to_all | solution.py:14
  98.4 0.8 broadcast_in_dim.140
  99.2 3.5 %all-to-all-start.1 = ((bf16[4,128,512]{2,1,0:T(8,128)(2,1)}), bf16[4,128,512]{2,1,0:T(8,128)(2,1)S(1)}, u32[]{:S(2)}, u32[]{:S(2)}) async-start(bf16[4,128,512]{2,1,0:T(8,128)(2,1)} %broadcast_in_dim.140), calls=%async_computation.1 | async-start | bytes 1048576 | tf_op jit(solution)/shard_map/all_to_all | solution.py:14
  103.4 0.1 broadcast_in_dim.144
  103.5 14.3 %all-to-all-done.1 = bf16[4,128,512]{2,1,0:T(8,128)(2,1)S(1)} async-done(((bf16[4,128,512]{2,1,0:T(8,128)(2,1)}), bf16[4,128,512]{2,1,0:T(8,128)(2,1)S(1)}, u32[]{:S(2)}, u32[]{:S(2)}) %all-to-all-start.1) | async-done | bytes 524320 | tf_op jit(solution)/shard_map/all_to_all | solution.py:14
  117.8 0.0 copy-start.2
  117.8 3.6 %fusion.10 = (f32[1024]{0:T(1024)S(1)}, f32[512]{0:T(512)S(1)}, f32[512,1024]{1,0:T(8,128)}) fusion(bf16[512,512]{1,0:T(8,128)(2,1)S(1)} %bitcast.34, bf16[1024,512]{1,0:T(8,128)(2,1)} %bitcast.2, f32[]{:T(128)} %bitcast.29), kind=kOutput, calls=%fused_computation.42 | convolution fusion | flops 538442240 | bytes 3676164 | tf_op jit(solution)/shard_map/dot_general | solution.py:52
  121.4 0.1 broadcast_select_fusion.1
  121.5 0.2 broadcast_in_dim.151
  121.7 0.8 broadcast_select_fusion
  122.5 4.8 %all-to-all-start.3 = ((f32[32,1,1024]{2,1,0:T(1,128)}), f32[32,1,1024]{2,1,0:T(1,128)S(1)}, u32[]{:S(2)}, u32[]{:S(2)}) async-start(f32[32,1,1024]{2,1,0:T(1,128)} %broadcast_select_fusion), calls=%async_computation.3 | async-start | bytes 262144 | tf_op jit(solution)/shard_map/all_to_all | solution.py:63
  127.3 0.1 and.42
  127.4 0.1 and.39
  127.5 0.1 and.40
  127.6 12.1 %all-to-all-done.3 = f32[32,1,1024]{2,1,0:T(1,128)S(1)} async-done(((f32[32,1,1024]{2,1,0:T(1,128)}), f32[32,1,1024]{2,1,0:T(1,128)S(1)}, u32[]{:S(2)}, u32[]{:S(2)}) %all-to-all-start.3) | async-done | bytes 131104 | tf_op jit(solution)/shard_map/all_to_all | solution.py:63
  139.7 0.1 fusion.7
  139.8 0.0 copy-done.2
  139.8 2.2 subtract_convert_fusion
  142.1 3.1 %fusion.11 = (bf16[512,512]{1,0:T(8,128)(2,1)}, f32[512,512]{1,0:T(8,128)}) fusion(bf16[512,1024]{1,0:T(8,128)(2,1)S(1)} %subtract_convert_fusion, bf16[1024,512]{1,0:T(8,128)(2,1)} %bitcast.2), kind=kOutput, calls=%fused_computation.43 | convolution fusion | flops 537133056 | bytes 3670016 | tf_op jit(solution)/shard_map/dot_general | solution.py:75
  145.2 4.1 %all-to-all-start.4 = ((bf16[4,128,512]{2,1,0:T(8,128)(2,1)}), bf16[4,128,512]{2,1,0:T(8,128)(2,1)}, u32[]{:S(2)}, u32[]{:S(2)}) async-start(bf16[4,128,512]{2,1,0:T(8,128)(2,1)} %bitcast.36), calls=%async_computation.4 | async-start | bytes 1048576 | tf_op jit(solution)/shard_map/all_to_all | solution.py:79
  149.4 3.5 %fusion.12 = (bf16[1024,512]{1,0:T(8,128)(2,1)}, f32[1024,512]{1,0:T(8,128)}) fusion(bf16[512,1024]{1,0:T(8,128)(2,1)S(1)} %subtract_convert_fusion, bf16[512,512]{1,0:T(8,128)(2,1)} %bitcast.35), kind=kOutput, calls=%fused_computation.44 | convolution fusion | flops 537395200 | bytes 4718592 | tf_op jit(solution)/shard_map/dot_general | solution.py:76
  152.8 0.0 copy-start.1
  152.8 9.6 %all-to-all-done.4 = bf16[4,128,512]{2,1,0:T(8,128)(2,1)} async-done(((bf16[4,128,512]{2,1,0:T(8,128)(2,1)}), bf16[4,128,512]{2,1,0:T(8,128)(2,1)}, u32[]{:S(2)}, u32[]{:S(2)}) %all-to-all-start.4) | async-done | bytes 524320 | tf_op jit(solution)/shard_map/all_to_all | solution.py:79
  162.4 4.2 %all-to-all-start.5 = ((bf16[8,128,512]{2,1,0:T(8,128)(2,1)}), bf16[8,128,512]{2,1,0:T(8,128)(2,1)}, u32[]{:S(2)}, u32[]{:S(2)}) async-start(bf16[8,128,512]{2,1,0:T(8,128)(2,1)} %bitcast.33), calls=%async_computation.5 | async-start | bytes 2097152 | tf_op jit(solution)/shard_map/all_to_all | solution.py:82
  166.7 1.3 select_reduce_fusion.1
  168.0 0.0 copy-done.1
  168.0 0.1 multiply_reduce_fusion
  168.1 0.1 subtract_convert_fusion.1
  168.3 0.0 copy-start.4
  168.3 0.6 copy-done.4
  168.9 1.7 fusion
  170.6 1.7 copy.8
  172.3 1.3 reshape.216
  173.6 19.0 %all-to-all-done.5 = bf16[8,128,512]{2,1,0:T(8,128)(2,1)} async-done(((bf16[8,128,512]{2,1,0:T(8,128)(2,1)}), bf16[8,128,512]{2,1,0:T(8,128)(2,1)}, u32[]{:S(2)}, u32[]{:S(2)}) %all-to-all-start.5) | async-done | bytes 1048608 | tf_op jit(solution)/shard_map/all_to_all | solution.py:82
  192.6 5.3 %all-to-all-start.6 = ((bf16[32,44,512]{2,1,0:T(8,128)(2,1)}), bf16[32,44,512]{2,1,0:T(8,128)(2,1)S(1)}, u32[]{:S(2)}, u32[]{:S(2)}) async-start(bf16[32,44,512]{2,1,0:T(8,128)(2,1)} %reshape.216), calls=%async_computation.6 | async-start | bytes 3145728 | tf_op jit(solution)/shard_map/all_to_all | solution.py:90
  197.9 2.3 convolution_convert_fusion.1
  200.2 1.5 select_reduce_fusion
  201.7 1.1 fusion.6
  202.8 1.7 fusion.5
  204.5 33.8 %all-to-all-done.6 = bf16[32,44,512]{2,1,0:T(8,128)(2,1)S(1)} async-done(((bf16[32,44,512]{2,1,0:T(8,128)(2,1)}), bf16[32,44,512]{2,1,0:T(8,128)(2,1)S(1)}, u32[]{:S(2)}, u32[]{:S(2)}) %all-to-all-start.6) | async-done | bytes 1441824 | tf_op jit(solution)/shard_map/all_to_all | solution.py:90
  238.3 0.9 convert_reduce_fusion
  (15 shorter events, 0.1 us)
Async XLA Ops:
  0.6 69.1 %copy-start = (bf16[128,1408]{1,0:T(8,128)(2,1)S(1)}, bf16[128,1408]{1,0:T(8,128)(2,1)}, u32[]{:S(2)}) copy-start(bf16[128,1408]{1,0:T(8,128)(2,1)} %param.4) | copy-start | bytes 1081348
  0.6 18.2 %copy-start.3 = (bf16[128,512]{1,0:T(8,128)(2,1)S(1)}, bf16[128,512]{1,0:T(8,128)(2,1)}, u32[]{:S(2)}) copy-start(bf16[128,512]{1,0:T(8,128)(2,1)} %param.5) | copy-start | bytes 393220
  2.8 56.6 %all-to-all-start = ((bf16[32,44,512]{2,1,0:T(8,128)(2,1)}), bf16[32,44,512]{2,1,0:T(8,128)(2,1)S(1)}, u32[]{:S(2)}, u32[]{:S(2)}) async-start(bf16[32,44,512]{2,1,0:T(8,128)(2,1)} %broadcast_in_dim.137), calls=%async_computation | async-start | bytes 3145728 | tf_op jit(solution)/shard_map/all_to_all | solution.py:14
  60.6 37.8 %all-to-all-start.2 = ((bf16[8,128,512]{2,1,0:T(8,128)(2,1)}), bf16[8,128,512]{2,1,0:T(8,128)(2,1)}, u32[]{:S(2)}, u32[]{:S(2)}) async-start(bf16[8,128,512]{2,1,0:T(8,128)(2,1)} %broadcast_in_dim.141), calls=%async_computation.2 | async-start | bytes 2097152 | tf_op jit(solution)/shard_map/all_to_all | solution.py:14
  99.2 18.6 %all-to-all-start.1 = ((bf16[4,128,512]{2,1,0:T(8,128)(2,1)}), bf16[4,128,512]{2,1,0:T(8,128)(2,1)S(1)}, u32[]{:S(2)}, u32[]{:S(2)}) async-start(bf16[4,128,512]{2,1,0:T(8,128)(2,1)} %broadcast_in_dim.140), calls=%async_computation.1 | async-start | bytes 1048576 | tf_op jit(solution)/shard_map/all_to_all | solution.py:14
  117.8 22.0 %copy-start.2 = (bf16[4,128,512]{2,1,0:T(8,128)(2,1)}, bf16[4,128,512]{2,1,0:T(8,128)(2,1)S(1)}, u32[]{:S(2)}) copy-start(bf16[4,128,512]{2,1,0:T(8,128)(2,1)S(1)} %all-to-all-done.1) | copy-start | bytes 1572868
  122.5 17.2 %all-to-all-start.3 = ((f32[32,1,1024]{2,1,0:T(1,128)}), f32[32,1,1024]{2,1,0:T(1,128)S(1)}, u32[]{:S(2)}, u32[]{:S(2)}) async-start(f32[32,1,1024]{2,1,0:T(1,128)} %broadcast_select_fusion), calls=%async_computation.3 | async-start | bytes 262144 | tf_op jit(solution)/shard_map/all_to_all | solution.py:63
  145.2 17.2 %all-to-all-start.4 = ((bf16[4,128,512]{2,1,0:T(8,128)(2,1)}), bf16[4,128,512]{2,1,0:T(8,128)(2,1)}, u32[]{:S(2)}, u32[]{:S(2)}) async-start(bf16[4,128,512]{2,1,0:T(8,128)(2,1)} %bitcast.36), calls=%async_computation.4 | async-start | bytes 1048576 | tf_op jit(solution)/shard_map/all_to_all | solution.py:79
  152.8 15.1 %copy-start.1 = (f32[512,512]{1,0:T(8,128)S(1)}, f32[512,512]{1,0:T(8,128)}, u32[]{:S(2)}) copy-start(f32[512,512]{1,0:T(8,128)} %get-tuple-element.15) | copy-start | bytes 3145732
  162.4 30.1 %all-to-all-start.5 = ((bf16[8,128,512]{2,1,0:T(8,128)(2,1)}), bf16[8,128,512]{2,1,0:T(8,128)(2,1)}, u32[]{:S(2)}, u32[]{:S(2)}) async-start(bf16[8,128,512]{2,1,0:T(8,128)(2,1)} %bitcast.33), calls=%async_computation.5 | async-start | bytes 2097152 | tf_op jit(solution)/shard_map/all_to_all | solution.py:82
  168.3 0.7 copy-start.4
  192.6 45.8 %all-to-all-start.6 = ((bf16[32,44,512]{2,1,0:T(8,128)(2,1)}), bf16[32,44,512]{2,1,0:T(8,128)(2,1)S(1)}, u32[]{:S(2)}, u32[]{:S(2)}) async-start(bf16[32,44,512]{2,1,0:T(8,128)(2,1)} %reshape.216), calls=%async_computation.6 | async-start | bytes 3145728 | tf_op jit(solution)/shard_map/all_to_all | solution.py:90
